TPU v7x, 32 devices: a whole 2x2x4 slice. The times are simulated.
32 devices in a mesh: gx: 8 (over z, y), gy: 4 (over x, core).
Axes of the slice: x: 2, y: 2, z: 4, core: 2. Of those that a mesh axis runs over, the one named last changes fastest.
Arguments:
- state: float32 [4, 5, 5, 64, 1024], P(None, None, None, 'gy', 'gx'), may hold values from -3 to 60, as said below
Outputs:
- advanced: float32 [4, 5, 5, 64, 1024], P(None, None, None, 'gy', 'gx')
- tendency: float32 [4, 5, 5, 64, 1024], P(None, None, None, 'gy', 'gx')
Inputs may be any that keep to these rules, and one draw needn't show every extreme that they name: `state`: at every node density is at least 0.2 and pressure, 0.4 times (energy minus half the squared momentum over density), is at least 0.2.
All inputs are finite; a program needn't handle non-finite values.
Results may differ from a plain program's by a relative error of at most 0.0003.
Values sent between devices are 32-bit elements; how exact they have to be, the bound alone decides.
A program may use at most 128 MiB of HBM per device.

v0:
```python
import math

import jax
import jax.numpy as jnp
import numpy as np
from jax import lax
from jax.sharding import PartitionSpec as P

ADIABATIC = 1.4
COURANT = 0.2
ALPHA_MAX = 0.5


def with_halo(cells, sides, width):
    for axis, dim in sides:
        count = lax.axis_size(axis)
        head = lax.slice_in_dim(cells, 0, width, axis=dim)
        tail = lax.slice_in_dim(cells, cells.shape[dim] - width, cells.shape[dim], axis=dim)
        cells = jnp.concatenate(
            [
                lax.ppermute(tail, axis, [(i, (i + 1) % count) for i in range(count)]),
                cells,
                lax.ppermute(head, axis, [((i + 1) % count, i) for i in range(count)]),
            ],
            axis=dim,
        )
    return cells


def tables():
    lobatto = np.array([-1.0, -math.sqrt(3.0 / 7.0), 0.0, math.sqrt(3.0 / 7.0), 1.0])
    weights = np.array([0.1, 49.0 / 90.0, 32.0 / 45.0, 49.0 / 90.0, 0.1])
    identity = np.eye(5)
    distance = lobatto[:, None] - lobatto[None, :] + identity
    barycentric = 1.0 / np.prod(distance, axis=1)
    derivative = (1.0 - identity) * (barycentric[None, :] / barycentric[:, None]) / distance
    derivative = derivative - identity * derivative.sum(axis=1)[:, None]
    legendre = np.zeros((5, 5))
    legendre[:, 0] = 1.0
    legendre[:, 1] = lobatto
    for degree in range(2, 5):
        legendre[:, degree] = (
            (2 * degree - 1) * lobatto * legendre[:, degree - 1]
            - (degree - 1) * legendre[:, degree - 2]
        ) / degree
    norms = np.array([2.0, 2.0 / 3.0, 2.0 / 5.0, 2.0 / 7.0, 0.5])
    inverse = (legendre * weights[:, None]).T / norms[:, None]
    levels = np.maximum(np.arange(5)[:, None], np.arange(5)[None, :])
    return (
        jnp.asarray(derivative, jnp.float32),
        jnp.asarray(weights, jnp.float32),
        jnp.asarray(inverse, jnp.float32),
        jnp.asarray(levels == 4, jnp.float32),
        jnp.asarray(levels == 3, jnp.float32),
        jnp.asarray(levels <= 3, jnp.float32),
    )


def slice_of(source, along_dim, begin_at, end_at):
    return lax.slice_in_dim(source, begin_at, end_at, axis=along_dim)


def slice_all(fields, along_dim, begin_at, end_at):
    return tuple((slice_of(member, along_dim, begin_at, end_at) for member in fields))


def primitive(conserved):
    density = conserved[0]
    speed_first = conserved[1] / density
    speed_second = conserved[2] / density
    pressure = (ADIABATIC - 1.0) * (
        conserved[3] - 0.5 * density * (speed_first * speed_first + speed_second * speed_second)
    )
    return (density, speed_first, speed_second, pressure)


def log_mean(left_val, right_val):
    relative = (left_val * (left_val - 2.0 * right_val) + right_val * right_val) / (
        left_val * (left_val + 2.0 * right_val) + right_val * right_val
    )
    nearby = relative < 0.0001
    series = (
        (left_val + right_val)
        * 52.5
        / (105.0 + relative * (35.0 + relative * (21.0 + relative * 15.0)))
    )
    logged = jnp.where(nearby, 1.0, jnp.log(right_val / left_val))
    return jnp.where(nearby, series, (right_val - left_val) / logged)


def two_point(left_state, right_state, normal_dir):
    mean_density = log_mean(left_state[0], right_state[0])
    thermal_mean = (
        left_state[3]
        * right_state[3]
        / log_mean(left_state[0] * right_state[3], right_state[0] * left_state[3])
    )
    mean_first = 0.5 * (left_state[1] + right_state[1])
    mean_second = 0.5 * (left_state[2] + right_state[2])
    mean_pressure = 0.5 * (left_state[3] + right_state[3])
    square_mean = 0.5 * (left_state[1] * right_state[1] + left_state[2] * right_state[2])
    left_normal = left_state[1 + normal_dir]
    right_normal = right_state[1 + normal_dir]
    mass_flux = mean_density * 0.5 * (left_normal + right_normal)
    push_first = mass_flux * mean_first + (mean_pressure if normal_dir == 0 else 0.0)
    push_second = mass_flux * mean_second + (mean_pressure if normal_dir == 1 else 0.0)
    energy_flux = mass_flux * (square_mean + thermal_mean / (ADIABATIC - 1.0)) + 0.5 * (
        left_state[3] * right_normal + right_state[3] * left_normal
    )
    return jnp.stack(jnp.broadcast_arrays(mass_flux, push_first, push_second, energy_flux))


def physical(primitives, normal_dir):
    normal_speed = primitives[1 + normal_dir]
    mass_flux = primitives[0] * normal_speed
    energy = primitives[3] / (ADIABATIC - 1.0) + 0.5 * primitives[0] * (
        primitives[1] * primitives[1] + primitives[2] * primitives[2]
    )
    push_first = mass_flux * primitives[1] + (primitives[3] if normal_dir == 0 else 0.0)
    push_second = mass_flux * primitives[2] + (primitives[3] if normal_dir == 1 else 0.0)
    return jnp.stack([mass_flux, push_first, push_second, normal_speed * (energy + primitives[3])])


def wave(primitives, normal_dir):
    return jnp.abs(primitives[1 + normal_dir]) + jnp.sqrt(ADIABATIC * primitives[3] / primitives[0])


def direction_block(
    conserved, primitives, normal_dir, before_trace, after_trace, derivative, weights
):
    node_dim = 1 if normal_dir == 0 else 0
    flux_dim = node_dim + 1
    cell_dim = 4 if normal_dir == 0 else 3
    elem_count = conserved.shape[cell_dim]
    shaper = [1, 1, 1, 1, 1]
    shaper[flux_dim] = 5
    volume = jnp.zeros(conserved.shape, jnp.float32)
    for partner in range(5):
        pair_flux = two_point(
            primitives, slice_all(primitives, node_dim, partner, partner + 1), normal_dir
        )
        volume = volume + (2.0 * derivative[:, partner]).reshape(tuple(shaper)) * pair_flux
    upper_trace = slice_of(conserved, flux_dim, 4, 5)
    lower_trace = slice_of(conserved, flux_dim, 0, 1)
    left_side = jnp.concatenate([before_trace, upper_trace], axis=cell_dim)
    right_side = jnp.concatenate([lower_trace, after_trace], axis=cell_dim)
    left_prims = primitive(left_side)
    right_prims = primitive(right_side)
    fastest = jnp.maximum(wave(left_prims, normal_dir), wave(right_prims, normal_dir))
    face_flux = two_point(left_prims, right_prims, normal_dir) - 0.5 * fastest * (
        right_side - left_side
    )
    flux_before = slice_of(face_flux, cell_dim, 0, elem_count)
    flux_after = slice_of(face_flux, cell_dim, 1, elem_count + 1)
    own_flux = physical(primitives, normal_dir)
    middle = jnp.zeros_like(slice_of(own_flux, flux_dim, 0, 3))
    surface = jnp.concatenate(
        [
            -(flux_before - slice_of(own_flux, flux_dim, 0, 1)) / weights[0],
            middle,
            (flux_after - slice_of(own_flux, flux_dim, 4, 5)) / weights[4],
        ],
        axis=flux_dim,
    )
    high_order = -(volume + surface)
    spread = jnp.maximum(
        wave(slice_all(primitives, node_dim, 0, 4), normal_dir),
        wave(slice_all(primitives, node_dim, 1, 5), normal_dir),
    )
    subcell = 0.5 * (
        slice_of(own_flux, flux_dim, 0, 4) + slice_of(own_flux, flux_dim, 1, 5)
    ) - 0.5 * spread * (slice_of(conserved, flux_dim, 1, 5) - slice_of(conserved, flux_dim, 0, 4))
    wall_flux = jnp.concatenate([flux_before, subcell, flux_after], axis=flux_dim)
    weight_column = weights.reshape(tuple(shaper))
    low_order = (
        -(slice_of(wall_flux, flux_dim, 1, 6) - slice_of(wall_flux, flux_dim, 0, 5)) / weight_column
    )
    return (high_order, low_order)


def raw_indicator(primitives, table_set):
    inverse, top_mask, next_mask, lower_mask = (
        table_set[2],
        table_set[3],
        table_set[4],
        table_set[5],
    )
    indicator = primitives[0] * primitives[3]
    modal_coef = jnp.einsum(
        "ka,lb,abrc->klrc", inverse, inverse, indicator, precision=lax.Precision.HIGHEST
    )
    squares = modal_coef * modal_coef
    total_energy = jnp.sum(squares, axis=(0, 1))
    top_part = jnp.sum(squares * top_mask[:, :, None, None], axis=(0, 1))
    next_part = jnp.sum(squares * next_mask[:, :, None, None], axis=(0, 1))
    lower_part = jnp.sum(squares * lower_mask[:, :, None, None], axis=(0, 1))
    energy = jnp.maximum(top_part / total_energy, next_part / lower_part)
    threshold = 0.5 * 10.0 ** (-1.8 * 5.0**0.25)
    sharpness = math.log((1.0 - 0.0001) / 0.0001)
    sigmoid_val = 1.0 / (1.0 + jnp.exp(-sharpness / threshold * (energy - threshold)))
    return jnp.minimum(sigmoid_val, ALPHA_MAX)


def rate_block(conserved, primitives, capped, neighbours, table_set):
    before_x, after_x, left_raw, right_raw, before_y, after_y, below_raw, above_raw = neighbours
    derivative, weights = (table_set[0], table_set[1])
    high_columns, low_columns = direction_block(
        conserved, primitives, 0, before_x, after_x, derivative, weights
    )
    high_rows, low_rows = direction_block(
        conserved, primitives, 1, before_y, after_y, derivative, weights
    )
    below_rows = jnp.concatenate([below_raw, capped[:-1]], axis=0)
    above_rows = jnp.concatenate([capped[1:], above_raw], axis=0)
    left_cols = jnp.concatenate([left_raw, capped[:, :-1]], axis=1)
    right_cols = jnp.concatenate([capped[:, 1:], right_raw], axis=1)
    beside_all = jnp.maximum(
        jnp.maximum(below_rows, above_rows), jnp.maximum(left_cols, right_cols)
    )
    blend_factor = jnp.maximum(capped, 0.5 * beside_all)
    high_order = high_columns + high_rows
    low_order = low_columns + low_rows
    return (1.0 - blend_factor) * high_order + blend_factor * low_order


def section_rate(current, table_set):
    primitives = primitive(current)
    capped = raw_indicator(primitives, table_set)
    rows = current.shape[3]
    cols = current.shape[4]
    column_pack = jnp.stack(
        [
            jnp.concatenate([current[:, :, 0, :, 0].reshape(20, rows), capped[:, 0][None]], axis=0),
            jnp.concatenate(
                [current[:, :, 4, :, -1].reshape(20, rows), capped[:, -1][None]], axis=0
            ),
        ]
    )
    column_got = with_halo(column_pack, (("gx", 0),), 1)
    row_pack = jnp.stack(
        [
            jnp.concatenate([current[:, 0, :, 0, :].reshape(20, cols), capped[0, :][None]], axis=0),
            jnp.concatenate(
                [current[:, 4, :, -1, :].reshape(20, cols), capped[-1, :][None]], axis=0
            ),
        ]
    )
    row_got = with_halo(row_pack, (("gy", 0),), 1)
    neighbours = (
        column_got[0, :20].reshape(4, 5, rows)[:, :, None, :, None],
        column_got[3, :20].reshape(4, 5, rows)[:, :, None, :, None],
        column_got[0, 20][:, None],
        column_got[3, 20][:, None],
        row_got[0, :20].reshape(4, 5, cols)[:, None, :, None, :],
        row_got[3, :20].reshape(4, 5, cols)[:, None, :, None, :],
        row_got[0, 20][None, :],
        row_got[3, 20][None, :],
    )
    return rate_block(current, primitives, capped, neighbours, table_set)


def local(state):
    table_set = tables()
    primitives = primitive(state)
    local_top = jnp.max(
        jnp.sqrt(primitives[1] * primitives[1] + primitives[2] * primitives[2])
        + jnp.sqrt(ADIABATIC * primitives[3] / primitives[0])
    )
    global_top = lax.pmax(local_top, ("gx", "gy"))
    delta_time = COURANT * 2.0 / (9.0 * global_top)
    rate_first = section_rate(state, table_set)
    first_state = state + delta_time * rate_first
    rate_second = section_rate(first_state, table_set)
    advanced = 0.5 * state + 0.5 * (first_state + delta_time * rate_second)
    return (advanced, rate_second)


def solution(mesh):
    placed = (P(None, None, None, "gy", "gx"),)
    return jax.shard_map(
        local,
        mesh=mesh,
        in_specs=placed,
        out_specs=(P(None, None, None, "gy", "gx"), P(None, None, None, "gy", "gx")),
        check_vma=False,
    )
```

profile of v0, /device:TPU:0, one launch (start us, length us, event | category | flops | bytes accessed | tf_op | source)
XLA Modules:
  0.0 163.4 jit_solution(17677989262511839350)
XLA Ops:
  1.7 2.1 %add_reduce_fusion = (f32[]{:T(128)}, f32[5,5,16,128]{3,2,1,0:T(8,128)S(1)}, f32[5,5,16,128]{3,2,1,0:T(8,128)S(1)}) fusion(f32[4,5,5,16,128]{4,3,2,1,0:T(8,128)} %param.7), kind=kLoop, calls=%fused_computation.584 | loop fusion | flops 614399 | bytes 1228804 | tf_op jit(solution)/shard_map/reduce_max | solution.py:265
  6.5 2.4 %collective-permute-start.1 = (f32[1,21,128]{2,1,0:T(8,128)}, f32[1,21,128]{2,1,0:T(8,128)}, u32[]{:S(2)}, u32[]{:S(2)}) collective-permute-start(f32[1,21,128]{2,1,0:T(8,128)} %maximum_bitcast_fusion.1), channel_id=1, source_target_pairs={{1,0},{2,1},{3,2},{0,3},{5,4},{6,5},{7,6},{4,7},{9,8},{10,9},{11,1... | collective-permute-start | bytes 32264 | tf_op jit(solution)/shard_map/ppermute | solution.py:23
  10.6 4.6 %collective-permute-start.3 = (f32[1,21,16]{2,1,0:T(8,128)}, f32[1,21,16]{2,1,0:T(8,128)}, u32[]{:S(2)}, u32[]{:S(2)}) collective-permute-start(f32[1,21,16]{2,1,0:T(8,128)} %maximum_bitcast_fusion.3), channel_id=1, source_target_pairs={{4,0},{8,4},{12,8},{16,12},{20,16},{24,20},{28,24},{0,28},{5,1},{9... | collective-permute-start | bytes 4040 | tf_op jit(solution)/shard_map/ppermute | solution.py:23
  20.0 1.4 multiply_multiply_fusion.58
  21.4 1.4 multiply_multiply_fusion.46
  22.7 1.4 multiply_multiply_fusion.54
  24.1 1.3 multiply_add_fusion.35
  28.1 1.2 multiply_add_fusion.54
  36.9 40.0 %pmax.7 = f32[]{:T(128)} all-reduce(f32[]{:T(128)} %get-tuple-element.70), channel_id=1, replica_groups=mesh['gx'=8,'gy'=4] {'gx','gy'}, use_global_device_ids=true, to_apply=%region_1.0 | all-reduce | flops 1 | bytes 8 | tf_op jit(solution)/shard_map/pmax | solution.py:269
  89.5 3.6 %fusion.12 = f32[4,5,5,16,128]{4,3,2,1,0:T(8,128)S(1)} fusion(f32[4,5,5,16,128]{4,3,2,1,0:T(8,128)S(1)} %copy-done, f32[1,5,5,16,128]{4,3,2,1,0:T(8,128)} %get-tuple-element.239, f32[1,5,5,16,128]{4,3,2,1,0:T(8,128)} %get-tuple-element.238, f32[1,5,5,16,128]{4,3,2,1,0:T(8,128)} %get-tuple-element.149, f32[1,5,5,16,128]{4,3,2,1,0:T(8,128)S(1)} %copy-done.46, ...), kind=kLoop, calls=%fused_computation.15 | loop fusion | flops 14950400 | bytes 12468368 | tf_op jit(solution)/shard_map/add | solution.py:272
  111.2 1.3 reshape_squeeze.30
  113.1 1.3 reshape_squeeze.28
  115.7 1.3 maximum_bitcast_fusion.5
  118.4 2.9 %collective-permute-start.7 = (f32[1,21,16]{2,1,0:T(8,128)S(1)}, f32[1,21,16]{2,1,0:T(8,128)}, u32[]{:S(2)}, u32[]{:S(2)}) collective-permute-start(f32[1,21,16]{2,1,0:T(8,128)S(1)} %maximum_bitcast_fusion.7), channel_id=1, source_target_pairs={{4,0},{8,4},{12,8},{16,12},{20,16},{24,20},{28,24},{0,28},{5,1},{9... | collective-permute-start | bytes 4040 | tf_op jit(solution)/shard_map/ppermute | solution.py:23
  121.6 2.2 %multiply_add_fusion.31 = (f32[1,5,5,16,128]{4,3,2,1,0:T(8,128)}, f32[1,5,5,16,128]{4,3,2,1,0:T(8,128)S(1)}, f32[1,5,5,16,128]{4,3,2,1,0:T(8,128)S(1)}, f32[1,5,...) fusion(f32[1,5,5,16,128]{4,3,2,1,0:T(8,128)S(1)} %get-tuple-element.38, ...), kind=kLoop, calls=%fused_computation.487 | loop fusion | flops 3481600 | bytes 2662400 | tf_op jit(solution)/shard_map/add | solution.py:105
  126.6 1.3 multiply_add_fusion.28
  131.9 1.3 multiply_add_fusion.25
  133.3 1.4 multiply_multiply_fusion.2
  136.0 1.4 multiply_multiply_fusion.6
  137.5 1.2 multiply_add_fusion.6
  140.1 1.4 multiply_multiply_fusion.18
  142.9 1.4 multiply_multiply_fusion.10
  144.3 1.4 multiply_add_fusion.9
  158.7 4.6 %add_multiply_fusion = (f32[4,5,5,16,128]{4,3,2,1,0:T(8,128)}, f32[4,5,5,16,128]{4,3,2,1,0:T(8,128)}) fusion(f32[4,5,5,16,128]{4,3,2,1,0:T(8,128)S(1)} %copy-done, f32[4,5,5,16,128]{4,3,2,1,0:T(8,128)S(1)} %fusion.12, f32[]{:T(128)S(6)} %div.2015, f32[5]{0:T(128)S(1)} %copy-done.179, f32[4,4,5,16,128]{4,3,2,1,0:T(8,128)S(1)} %copy-done.7, ...), kind=kLoop, calls=%fused_computation.76 | loop fusion | flops 15360000 | bytes 14106768 | tf_op jit(solution)/shard_map/add | solution.py:274
  (531 shorter events, 76.2 us)
Async XLA Ops:
  6.5 77.3 %collective-permute-start.1 = (f32[1,21,128]{2,1,0:T(8,128)}, f32[1,21,128]{2,1,0:T(8,128)}, u32[]{:S(2)}, u32[]{:S(2)}) collective-permute-start(f32[1,21,128]{2,1,0:T(8,128)} %maximum_bitcast_fusion.1), channel_id=1, source_target_pairs={{1,0},{2,1},{3,2},{0,3},{5,4},{6,5},{7,6},{4,7},{9,8},{10,9},{11,1... | collective-permute-start | bytes 32264 | tf_op jit(solution)/shard_map/ppermute | solution.py:23
  9.5 75.1 %collective-permute-start = (f32[1,21,128]{2,1,0:T(8,128)}, f32[1,21,128]{2,1,0:T(8,128)}, u32[]{:S(2)}, u32[]{:S(2)}) collective-permute-start(f32[1,21,128]{2,1,0:T(8,128)} %maximum_bitcast_fusion), channel_id=1, source_target_pairs={{0,1},{1,2},{2,3},{3,0},{4,5},{5,6},{6,7},{7,4},{8,9},{9,10},{10,1... | collective-permute-start | bytes 32264 | tf_op jit(solution)/shard_map/ppermute | solution.py:21
  10.6 68.4 %collective-permute-start.3 = (f32[1,21,16]{2,1,0:T(8,128)}, f32[1,21,16]{2,1,0:T(8,128)}, u32[]{:S(2)}, u32[]{:S(2)}) collective-permute-start(f32[1,21,16]{2,1,0:T(8,128)} %maximum_bitcast_fusion.3), channel_id=1, source_target_pairs={{4,0},{8,4},{12,8},{16,12},{20,16},{24,20},{28,24},{0,28},{5,1},{9... | collective-permute-start | bytes 4040 | tf_op jit(solution)/shard_map/ppermute | solution.py:23
  15.8 62.4 %collective-permute-start.2 = (f32[1,21,16]{2,1,0:T(8,128)}, f32[1,21,16]{2,1,0:T(8,128)}, u32[]{:S(2)}, u32[]{:S(2)}) collective-permute-start(f32[1,21,16]{2,1,0:T(8,128)} %maximum_bitcast_fusion.2), channel_id=1, source_target_pairs={{0,4},{4,8},{8,12},{12,16},{16,20},{20,24},{24,28},{28,0},{1,5},{5... | collective-permute-start | bytes 4040 | tf_op jit(solution)/shard_map/ppermute | solution.py:21
  16.4 10.7 %copy-start.31 = (f32[1,5,5,16,128]{4,3,2,1,0:T(8,128)}, f32[1,5,5,16,128]{4,3,2,1,0:T(8,128)S(1)}, u32[]{:S(2)}) copy-start(f32[1,5,5,16,128]{4,3,2,1,0:T(8,128)S(1)} %get-tuple-element.82) | copy-start | bytes 614404
  18.9 8.2 %copy-start.37 = (f32[1,5,5,16,128]{4,3,2,1,0:T(8,128)}, f32[1,5,5,16,128]{4,3,2,1,0:T(8,128)S(1)}, u32[]{:S(2)}) copy-start(f32[1,5,5,16,128]{4,3,2,1,0:T(8,128)S(1)} %get-tuple-element.86) | copy-start | bytes 614404
  20.0 15.1 %copy-start.33 = (f32[1,5,5,16,128]{4,3,2,1,0:T(8,128)}, f32[1,5,5,16,128]{4,3,2,1,0:T(8,128)S(1)}, u32[]{:S(2)}) copy-start(f32[1,5,5,16,128]{4,3,2,1,0:T(8,128)S(1)} %get-tuple-element.140) | copy-start | bytes 614404
  96.2 27.7 %copy-start.3 = (f32[1,5,5,16,128]{4,3,2,1,0:T(8,128)}, f32[1,5,5,16,128]{4,3,2,1,0:T(8,128)S(1)}, u32[]{:S(2)}) copy-start(f32[1,5,5,16,128]{4,3,2,1,0:T(8,128)S(1)} %get-tuple-element.34) | copy-start | bytes 614404
  96.2 27.7 %copy-start.29 = (f32[1,5,5,16,128]{4,3,2,1,0:T(8,128)}, f32[1,5,5,16,128]{4,3,2,1,0:T(8,128)S(1)}, u32[]{:S(2)}) copy-start(f32[1,5,5,16,128]{4,3,2,1,0:T(8,128)S(1)} %get-tuple-element.33) | copy-start | bytes 614404
  96.4 27.6 %copy-start.23 = (f32[1,5,5,16,128]{4,3,2,1,0:T(8,128)}, f32[1,5,5,16,128]{4,3,2,1,0:T(8,128)S(1)}, u32[]{:S(2)}) copy-start(f32[1,5,5,16,128]{4,3,2,1,0:T(8,128)S(1)} %get-tuple-element.37) | copy-start | bytes 614404
  115.7 5.6 %copy-start.159 = (f32[20,16]{1,0:T(8,128)S(1)}, f32[20,16]{1,0:T(8,128)}, u32[]{:S(2)}) copy-start(f32[20,16]{1,0:T(8,128)} %reshape_squeeze.30) | copy-start | bytes 3844
  115.7 5.6 %copy-start.182 = (f32[16]{0:T(128)S(1)}, f32[16]{0:T(128)}, u32[]{:S(2)}) copy-start(f32[16]{0:T(128)} %get-tuple-element.18) | copy-start | bytes 196
  115.7 5.9 %copy-start.94 = (f32[5,16,128]{2,1,0:T(8,128)S(1)}, f32[5,16,128]{2,1,0:T(8,128)}, u32[]{:S(2)}) copy-start(f32[5,16,128]{2,1,0:T(8,128)} %get-tuple-element.330) | copy-start | bytes 122884
  117.0 4.6 %copy-start.93 = (f32[5,16,128]{2,1,0:T(8,128)S(1)}, f32[5,16,128]{2,1,0:T(8,128)}, u32[]{:S(2)}) copy-start(f32[5,16,128]{2,1,0:T(8,128)} %get-tuple-element.298) | copy-start | bytes 122884
  117.0 36.1 %collective-permute-start.5 = (f32[1,21,128]{2,1,0:T(8,128)}, f32[1,21,128]{2,1,0:T(8,128)}, u32[]{:S(2)}, u32[]{:S(2)}) collective-permute-start(f32[1,21,128]{2,1,0:T(8,128)} %maximum_bitcast_fusion.5), channel_id=1, source_target_pairs={{1,0},{2,1},{3,2},{0,3},{5,4},{6,5},{7,6},{4,7},{9,8},{10,9},{11,1... | collective-permute-start | bytes 32264 | tf_op jit(solution)/shard_map/ppermute | solution.py:23
  118.4 29.6 %collective-permute-start.7 = (f32[1,21,16]{2,1,0:T(8,128)S(1)}, f32[1,21,16]{2,1,0:T(8,128)}, u32[]{:S(2)}, u32[]{:S(2)}) collective-permute-start(f32[1,21,16]{2,1,0:T(8,128)S(1)} %maximum_bitcast_fusion.7), channel_id=1, source_target_pairs={{4,0},{8,4},{12,8},{16,12},{20,16},{24,20},{28,24},{0,28},{5,1},{9... | collective-permute-start | bytes 4040 | tf_op jit(solution)/shard_map/ppermute | solution.py:23
  121.3 25.2 %collective-permute-start.6 = (f32[1,21,16]{2,1,0:T(8,128)S(1)}, f32[1,21,16]{2,1,0:T(8,128)S(1)}, u32[]{:S(2)}, u32[]{:S(2)}) collective-permute-start(f32[1,21,16]{2,1,0:T(8,128)S(1)} %maximum_bitcast_fusion.6), channel_id=1, source_target_pairs={{0,4},{4,8},{8,12},{12,16},{16,20},{20,24},{24,28},{28,0},{1,5},{5... | collective-permute-start | bytes 4040 | tf_op jit(solution)/shard_map/ppermute | solution.py:21
  123.9 5.2 %copy-start.47 = (f32[1,5,5,16,128]{4,3,2,1,0:T(8,128)}, f32[1,5,5,16,128]{4,3,2,1,0:T(8,128)S(1)}, u32[]{:S(2)}) copy-start(f32[1,5,5,16,128]{4,3,2,1,0:T(8,128)S(1)} %get-tuple-element.125) | copy-start | bytes 614404
  123.9 14.9 %copy-start.11 = (f32[1,5,5,16,128]{4,3,2,1,0:T(8,128)}, f32[1,5,5,16,128]{4,3,2,1,0:T(8,128)S(1)}, u32[]{:S(2)}) copy-start(f32[1,5,5,16,128]{4,3,2,1,0:T(8,128)S(1)} %get-tuple-element.127) | copy-start | bytes 614404
  123.9 20.4 %copy-start.1 = (f32[1,5,5,16,128]{4,3,2,1,0:T(8,128)}, f32[1,5,5,16,128]{4,3,2,1,0:T(8,128)S(1)}, u32[]{:S(2)}) copy-start(f32[1,5,5,16,128]{4,3,2,1,0:T(8,128)S(1)} %get-tuple-element.69) | copy-start | bytes 614404
  146.3 7.5 %collective-permute-start.4 = (f32[1,21,128]{2,1,0:T(8,128)S(1)}, f32[1,21,128]{2,1,0:T(8,128)S(1)}, u32[]{:S(2)}, u32[]{:S(2)}) collective-permute-start(f32[1,21,128]{2,1,0:T(8,128)S(1)} %maximum_bitcast_fusion.4), channel_id=1, source_target_pairs={{0,1},{1,2},{2,3},{3,0},{4,5},{5,6},{6,7},{7,4},{8,9},{9,10},{10,1... | collective-permute-start | bytes 32264 | tf_op jit(solution)/shard_map/ppermute | solution.py:21
  154.4 3.6 %copy-start.59 = (f32[1,5,5,16,128]{4,3,2,1,0:T(8,128)S(1)}, f32[1,5,5,16,128]{4,3,2,1,0:T(8,128)}, u32[]{:S(2)}) copy-start(f32[1,5,5,16,128]{4,3,2,1,0:T(8,128)} %get-tuple-element.224) | copy-start | bytes 614404
  154.4 3.6 %copy-start.60 = (f32[1,5,5,16,128]{4,3,2,1,0:T(8,128)S(1)}, f32[1,5,5,16,128]{4,3,2,1,0:T(8,128)}, u32[]{:S(2)}) copy-start(f32[1,5,5,16,128]{4,3,2,1,0:T(8,128)} %get-tuple-element.225) | copy-start | bytes 614404
  154.4 3.6 %copy-start.61 = (f32[1,5,5,16,128]{4,3,2,1,0:T(8,128)S(1)}, f32[1,5,5,16,128]{4,3,2,1,0:T(8,128)}, u32[]{:S(2)}) copy-start(f32[1,5,5,16,128]{4,3,2,1,0:T(8,128)} %get-tuple-element.222) | copy-start | bytes 614404
  (176 other events, 260.8 us)
where the time goes:
time: 166 us; the launch traced here: 163 us
  other arithmetic  64.8 us (39%)
  local copies, waits for them, and re-layouts  41.6 us (25%)
  blocking collectives  40 us (24%)
  starting transfers between devices  11 us (7%)
  between operations  3.75 us (2%)
  matrix products  2.28 us (1%)
    pmax x1, blocking collectives, local(): global_top = lax.pmax(local_top, ('gx', 'gy'))  40 us
    unnamed x384, local copies, waits for them, and re-layouts  13.6 us
    mul x10, other arithmetic, two_point(): mass_flux * mean_first + (mean_pressure if normal_dir == 0 else 0.0)  11 us
    ppermute x4, starting transfers between devices, with_halo(): lax.ppermute(head, axis, [((i + 1) % count, i) for i in range(count)])  10.5 us
    add x8, other arithmetic, two_point(): mass_flux * mean_second + (mean_pressure if normal_dir == 1 else 0.0)  7.79 us
    add x7, other arithmetic, two_point(): mass_flux * mean_first + (mean_pressure if normal_dir == 0 else 0.0)  7.64 us
    mul x8, other arithmetic, two_point(): mass_flux * mean_second + (mean_pressure if normal_dir == 1 else 0.0)  7.32 us
    add x1, other arithmetic, local(): advanced = 0.5 * state + 0.5 * (first_state + delta_time * rate_second)  4.58 us
  transfers between devices with their start and end apart: 8, of which 0 were waited for; matrix products, arithmetic and copies ran while one was open for 33% of the time, Pallas kernels for 0%

commit v1 on v0

v1 whole, which is shorter than its diff:
```python
import functools
import math

import jax
import jax.numpy as jnp
import numpy as np
from jax import lax
from jax.experimental import pallas as pl
from jax.experimental.pallas import tpu as pltpu
from jax.sharding import PartitionSpec as P

MESH = pl.DeviceIdType.MESH
COURANT = 0.2
F32 = jnp.float32
LANES = 128
RHO, HX, HY, PR, LR, BE, LB, HC = range(8)


def tables():
    lobatto = np.array([-1.0, -math.sqrt(3.0 / 7.0), 0.0, math.sqrt(3.0 / 7.0), 1.0])
    weights = np.array([0.1, 49.0 / 90.0, 32.0 / 45.0, 49.0 / 90.0, 0.1])
    identity = np.eye(5)
    distance = lobatto[:, None] - lobatto[None, :] + identity
    barycentric = 1.0 / np.prod(distance, axis=1)
    derivative = (1.0 - identity) * (barycentric[None, :] / barycentric[:, None]) / distance
    legendre = np.zeros((5, 5))
    legendre[:, 0] = 1.0
    legendre[:, 1] = lobatto
    for degree in range(2, 5):
        legendre[:, degree] = (
            (2 * degree - 1) * lobatto * legendre[:, degree - 1]
            - (degree - 1) * legendre[:, degree - 2]
        ) / degree
    norms = np.array([2.0, 2.0 / 3.0, 2.0 / 5.0, 2.0 / 7.0, 0.5])
    inverse = (legendre * weights[:, None]).T / norms[:, None]
    return derivative, weights, inverse


DERIV, WEIGHTS, INVERSE = tables()
WINV = [float(1.0 / w) for w in WEIGHTS]


def coarse_inv(x):
    return pl.reciprocal(x, approx=True)


def inv(x):
    r = pl.reciprocal(x, approx=True)
    return r * (2.0 - x * r)


def series(f):
    return 2.0 + f * (2.0 / 3.0 + f * (2.0 / 5.0 + f * (2.0 / 7.0 + f * (2.0 / 9.0))))


def pair_flux(l, r, n):
    d = r[RHO] - l[RHO]
    s = r[RHO] + l[RHO]
    z = d * coarse_inv(s)
    f = z * z
    near = f < 0.03
    mean_rho = jnp.where(near, s, d) * inv(jnp.where(near, series(f), r[LR] - l[LR]))
    d2 = r[BE] - l[BE]
    s2 = r[BE] + l[BE]
    z2 = d2 * coarse_inv(s2)
    f2 = z2 * z2
    near2 = f2 < 0.03
    thermal = jnp.where(near2, series(f2), r[LB] - l[LB]) * inv(jnp.where(near2, s2, d2))
    hn, ht = (HX, HY) if n == 0 else (HY, HX)
    mass = mean_rho * (l[hn] + r[hn])
    normal = mass * (l[hn] + r[hn]) + 0.5 * (l[PR] + r[PR])
    tangent = mass * (l[ht] + r[ht])
    energy = mass * (2.0 * (l[HX] * r[HX] + l[HY] * r[HY]) + 2.5 * thermal) + (
        l[PR] * r[hn] + r[PR] * l[hn]
    )
    return (mass, normal, tangent, energy) if n == 0 else (mass, tangent, normal, energy)


def primitives_of(u):
    ri = inv(u[0])
    vx = u[1] * ri
    vy = u[2] * ri
    pressure = 0.4 * (u[3] - 0.5 * (u[1] * vx + u[2] * vy))
    beta = u[0] * inv(pressure)
    half_sound = jnp.sqrt(0.35 * pressure * ri)
    log_rho = jnp.log(u[0])
    log_beta = log_rho - jnp.log(pressure)
    return (u[0], 0.5 * vx, 0.5 * vy, pressure, log_rho, beta, log_beta, half_sound)


def face_of(l, r, el, er, n):
    flux = pair_flux(l, r, n)
    hn = HX if n == 0 else HY
    fast = jnp.maximum(jnp.abs(l[hn]) + l[HC], jnp.abs(r[hn]) + r[HC])
    fast2 = fast + fast
    return (
        flux[0] - fast * (r[RHO] - l[RHO]),
        flux[1] - fast2 * (r[RHO] * r[HX] - l[RHO] * l[HX]),
        flux[2] - fast2 * (r[RHO] * r[HY] - l[RHO] * l[HY]),
        flux[3] - fast * (er - el),
    )


def transform(values):
    v0, v1, v2, v3, v4 = values
    s0, s1, d0, d1 = v0 + v4, v1 + v3, v4 - v0, v3 - v1
    out = []
    for k in range(5):
        row = [float(c) for c in INVERSE[k]]
        if k % 2 == 0:
            out.append(row[0] * s0 + row[1] * s1 + row[2] * v2)
        else:
            out.append(row[4] * d0 + row[3] * d1)
    return out


def kernel(
    ngx, ngy, state, adv, tend,
    prim, first, rx, sx, fx, fy, raw, blend, packx, packy, gotx, goty,
    edge, top, top_got, top2, top2_got,
    hs, hr, ts, tr, t2s, t2r,
):
    gx = lax.axis_index("gx")
    gy = lax.axis_index("gy")
    at_x = lambda d: (lax.rem(gx + d, ngx), gy)
    at_y = lambda d: (gx, lax.rem(gy + d, ngy))
    rows = state.shape[2]
    halves = rows // 8

    barrier = pltpu.get_barrier_semaphore()
    for d in range(1, ngx):
        pl.semaphore_signal(barrier, inc=1, device_id=at_x(d), device_id_type=MESH)
    for d in range(1, ngy):
        pl.semaphore_signal(barrier, inc=1, device_id=at_y(d), device_id_type=MESH)

    lane = lax.broadcasted_iota(jnp.int32, (rows, LANES), 1)
    row = lax.broadcasted_iota(jnp.int32, (rows, LANES), 0)

    def tile(h):
        return pl.ds(pl.multiple_of(h * 8, 8), 8)

    def remote(src, dst, send, recv, device):
        return pltpu.make_async_remote_copy(
            src_ref=src, dst_ref=dst, send_sem=send, recv_sem=recv,
            device_id=device, device_id_type=MESH,
        )

    def halo_copies(sec):
        return [
            remote(packx.at[sec, 0], gotx.at[sec, 0], hs.at[sec, 0], hr.at[sec, 0], at_x(1)),
            remote(packx.at[sec, 1], gotx.at[sec, 1], hs.at[sec, 1], hr.at[sec, 1], at_x(ngx - 1)),
            remote(packy.at[sec, 0], goty.at[sec, 0], hs.at[sec, 2], hr.at[sec, 2], at_y(1)),
            remote(packy.at[sec, 1], goty.at[sec, 1], hs.at[sec, 3], hr.at[sec, 3], at_y(ngy - 1)),
        ]

    def indicator(sec):
        def body(h, carry):
            r = tile(h)
            lines = []
            for a in range(5):
                lines.append(
                    transform(
                        [prim[RHO, a * 5 + b, r, :] * prim[PR, a * 5 + b, r, :] for b in range(5)]
                    )
                )
            sums = {}
            for l in range(5):
                modes = transform([lines[a][l] for a in range(5)])
                for k in range(5):
                    level = max(k, l)
                    sq = modes[k] * modes[k]
                    key = level if level >= 3 else 0
                    sums[key] = sums[key] + sq if key in sums else sq
            lower = sums[0] + sums[3]
            total = lower + sums[4]
            level = jnp.maximum(sums[4] / total, sums[3] / lower)
            threshold = 0.5 * 10.0 ** (-1.8 * 5.0**0.25)
            sharp = math.log((1.0 - 0.0001) / 0.0001)
            value = 1.0 / (1.0 + jnp.exp((-sharp / threshold) * (level - threshold)))
            raw[r, :] = jnp.minimum(value, 0.5)
            return carry

        lax.fori_loop(0, halves, body, 0)

    def pack(sec, u):
        hi = jnp.where(lane == 5, pltpu.roll(raw[...], 6, 1), 0.0)
        lo = jnp.where(lane == 5, pltpu.roll(raw[...], 5, 1), 0.0)
        for v in range(4):
            for a in range(5):
                k = v * 8 + a
                hi = jnp.where(lane == k, pltpu.roll(u[v, a * 5 + 4], k + 1, 1), hi)
                low = u[v, a * 5]
                lo = jnp.where(lane == k, pltpu.roll(low, k, 1) if k else low, lo)
        packx[sec, 0] = hi
        packx[sec, 1] = lo
        packy[sec] = jnp.zeros(packy.shape[1:], F32)
        for v in range(4):
            for b in range(5):
                k = v * 8 + b
                packy[sec, 0, k : k + 1, :] = u[v, 20 + b, rows - 1 : rows, :]
                packy[sec, 1, k : k + 1, :] = u[v, b, 0:1, :]
        packy[sec, 0, 5:6, :] = raw[rows - 1 : rows, :]
        packy[sec, 1, 5:6, :] = raw[0:1, :]

    def faces(u):
        def body(i, carry):
            hi, lo = i * 5 + 4, i * 5
            l = [pltpu.roll(prim[q, hi], 1, 1) for q in range(8)]
            r = [prim[q, lo] for q in range(8)]
            flux = face_of(l, r, pltpu.roll(u[3, hi], 1, 1), u[3, lo], 0)
            for v in range(4):
                fx[i, 0, v] = flux[v]
                fx[i, 1, v] = pltpu.roll(flux[v], LANES - 1, 1)
            hi, lo = 20 + i, i
            l = [pltpu.roll(prim[q, hi], 1, 0) for q in range(8)]
            r = [prim[q, lo] for q in range(8)]
            flux = face_of(l, r, pltpu.roll(u[3, hi], 1, 0), u[3, lo], 1)
            for v in range(4):
                fy[i, 0, v] = flux[v]
                fy[i, 1, v] = pltpu.roll(flux[v], rows - 1, 0)
            return carry

        lax.fori_loop(0, 5, body, 0)

    def line_terms(n, node, r, u):
        def load(k):
            return [prim[q, node(k), r, :] for q in range(7)]

        acc = [[None] * 4 for _ in range(5)]
        for i in range(5):
            for j in range(i + 1, 5):
                q = float(2.0 * WEIGHTS[i] * DERIV[i, j])
                flux = pair_flux(load(i), load(j), n)
                for v in range(4):
                    term = q * flux[v]
                    acc[i][v] = term if acc[i][v] is None else acc[i][v] + term
                    acc[j][v] = -term if acc[j][v] is None else acc[j][v] - term
        hn = HX if n == 0 else HY

        def half(k):
            c = [u[v, node(k), r, :] for v in range(4)]
            speed = prim[hn, node(k), r, :]
            p = prim[PR, node(k), r, :]
            h = [0.5 * c[1 + n], speed * c[1], speed * c[2], speed * (c[3] + p)]
            h[1 + n] = h[1 + n] + 0.5 * p
            return c, h, jnp.abs(speed) + prim[HC, node(k), r, :]

        before = half(0)
        prev = None
        outs = []
        for k in range(5):
            if k < 4:
                after = half(k + 1)
                fast = jnp.maximum(before[2], after[2])
                g = [
                    before[1][v] + after[1][v] - fast * (after[0][v] - before[0][v])
                    for v in range(4)
                ]
                before = after
            for v in range(4):
                if k == 0:
                    t = g[v]
                elif k == 4:
                    t = -prev[v]
                else:
                    t = g[v] - prev[v]
                outs.append((k, v, acc[k][v] * -WINV[k], (acc[k][v] - t) * WINV[k]))
            prev = g
        return outs

    def volume_x(u):
        def body(i, carry):
            def inner(h, c):
                r = tile(h)
                for k, v, vol, diff in line_terms(0, lambda k: i * 5 + k, r, u):
                    rx[v, i * 5 + k, r, :] = vol
                    sx[v, i * 5 + k, r, :] = diff
                return c

            return lax.fori_loop(0, halves, inner, carry)

        lax.fori_loop(0, 5, body, 0)

    def finish_halo(sec):
        hi, lo = packx[sec, 0], packx[sec, 1]
        from_left, from_right = gotx[sec, 0], gotx[sec, 1]
        lslab = jnp.where(lane < 64, from_left, pltpu.roll(hi, 64, 1))
        rslab = jnp.where(lane < 64, lo, pltpu.roll(from_right, 64, 1))
        lu = [lslab if v == 0 else pltpu.roll(lslab, LANES - 8 * v, 1) for v in range(4)]
        ru = [rslab if v == 0 else pltpu.roll(rslab, LANES - 8 * v, 1) for v in range(4)]
        flux = face_of(primitives_of(lu), primitives_of(ru), lu[3], ru[3], 0)
        for a in range(5):
            for v in range(4):
                low = pltpu.roll(flux[v], LANES - a, 1) if a else flux[v]
                high = pltpu.roll(flux[v], 63 - a, 1)
                flo = jnp.where(lane == 0, low, fx[a, 0, v])
                fhi = jnp.where(lane == LANES - 1, high, fx[a, 1, v])
                rx[v, a * 5] = rx[v, a * 5] + WINV[0] * flo
                rx[v, a * 5 + 4] = rx[v, a * 5 + 4] - WINV[4] * fhi
        for side in range(2):
            lsrc = goty.at[sec, 0] if side == 0 else packy.at[sec, 0]
            rsrc = packy.at[sec, 1] if side == 0 else goty.at[sec, 1]
            lu = [lsrc[8 * v : 8 * v + 8, :] for v in range(4)]
            ru = [rsrc[8 * v : 8 * v + 8, :] for v in range(4)]
            flux = face_of(primitives_of(lu), primitives_of(ru), lu[3], ru[3], 1)
            for v in range(4):
                edge[side, v] = flux[v]
        for b in range(5):
            for v in range(4):
                fy[b, 0, v, 0:1, :] = edge[0, v, b : b + 1, :]
                fy[b, 1, v, rows - 1 : rows, :] = edge[1, v, b : b + 1, :]
        own = raw[...]
        left = jnp.where(lane == 0, pltpu.roll(from_left, LANES - 5, 1), pltpu.roll(own, 1, 1))
        right = jnp.where(
            lane == LANES - 1, pltpu.roll(from_right, LANES - 6, 1), pltpu.roll(own, LANES - 1, 1)
        )
        below = jnp.where(row == 0, goty[sec, 0, 5:6, :], pltpu.roll(own, 1, 0))
        above = jnp.where(row == rows - 1, goty[sec, 1, 5:6, :], pltpu.roll(own, rows - 1, 0))
        beside = jnp.maximum(jnp.maximum(left, right), jnp.maximum(below, above))
        blend[...] = jnp.maximum(own, 0.5 * beside)

    def volume_y(u, sink):
        def body(i, carry):
            def inner(h, c):
                r = tile(h)
                share = blend[r, :]
                for k, v, vol, diff in line_terms(1, lambda k: k * 5 + i, r, u):
                    m = k * 5 + i
                    rate = (rx[v, m, r, :] + vol) + share * (sx[v, m, r, :] + diff)
                    if k == 0:
                        rate = rate + WINV[0] * fy[i, 0, v, r, :]
                    if k == 4:
                        rate = rate - WINV[4] * fy[i, 1, v, r, :]
                    sink(v, m, r, rate)
                return c

            return lax.fori_loop(0, halves, inner, carry)

        lax.fori_loop(0, 5, body, 0)

    def prepare(m, fastest):
        q = primitives_of([state[v, m] for v in range(4)])
        for f in range(8):
            prim[f, m] = q[f]
        speed = jnp.sqrt(q[HX] * q[HX] + q[HY] * q[HY]) + q[HC]
        return jnp.maximum(fastest, speed)

    fastest = lax.fori_loop(0, 25, prepare, jnp.zeros((rows, LANES), F32))
    local_top = fastest[0:8]
    for h in range(1, halves):
        local_top = jnp.maximum(local_top, fastest[8 * h : 8 * h + 8])
    top[...] = local_top
    indicator(0)
    pack(0, state)
    pl.semaphore_wait(barrier, ngx + ngy - 2)
    halos = halo_copies(0)
    tops = [
        remote(top, top_got.at[d - 1], ts.at[d - 1], tr.at[d - 1], at_x(d)) for d in range(1, ngx)
    ]
    for copy in halos + tops:
        copy.start()
    faces(state)
    for copy in tops:
        copy.wait()
    local_top = top[...]
    for d in range(ngx - 1):
        local_top = jnp.maximum(local_top, top_got[d])
    top2[...] = local_top
    volume_x(state)
    tops = [
        remote(top2, top2_got.at[d - 1], t2s.at[d - 1], t2r.at[d - 1], at_y(d))
        for d in range(1, ngy)
    ]
    for copy in tops:
        copy.start()
    for copy in halos:
        copy.wait()
    finish_halo(0)

    def keep_rate(v, m, r, rate):
        tend[v, m, r, :] = rate

    volume_y(state, keep_rate)
    for copy in tops:
        copy.wait()
    local_top = top2[...]
    for d in range(ngy - 1):
        local_top = jnp.maximum(local_top, top2_got[d])
    step = (COURANT * 2.0 / 9.0) / (2.0 * jnp.max(local_top, keepdims=True))
    step = jnp.broadcast_to(step, (8, LANES))
    step_full = jnp.concatenate([step] * halves, axis=0)

    def prepare2(m, carry):
        u = [state[v, m] + step_full * tend[v, m] for v in range(4)]
        for v in range(4):
            first[v, m] = u[v]
        q = primitives_of(u)
        for f in range(8):
            prim[f, m] = q[f]
        return carry

    lax.fori_loop(0, 25, prepare2, 0)
    indicator(1)
    pack(1, first)
    faces(first)
    halos = halo_copies(1)
    for copy in halos:
        copy.start()
    volume_x(first)
    for copy in halos:
        copy.wait()
    finish_halo(1)

    def keep_both(v, m, r, rate):
        tend[v, m, r, :] = rate
        adv[v, m, r, :] = 0.5 * state[v, m, r, :] + 0.5 * (first[v, m, r, :] + step * rate)

    volume_y(first, keep_both)


def local(ngx, ngy, state):
    shape = state.shape
    rows, cols = shape[3], shape[4]
    flat = (4, 25, rows, cols)
    vmem = lambda *s: pltpu.VMEM(s, F32)
    out = pl.pallas_call(
        functools.partial(kernel, ngx, ngy),
        out_shape=(jax.ShapeDtypeStruct(flat, F32),) * 2,
        in_specs=[pl.BlockSpec(memory_space=pltpu.VMEM)],
        out_specs=[pl.BlockSpec(memory_space=pltpu.VMEM)] * 2,
        scratch_shapes=[
            vmem(8, 25, rows, cols),
            vmem(*flat), vmem(*flat), vmem(*flat),
            vmem(5, 2, 4, rows, cols), vmem(5, 2, 4, rows, cols),
            vmem(rows, cols), vmem(rows, cols),
            vmem(2, 2, rows, cols), vmem(2, 2, 32, cols),
            vmem(2, 2, rows, cols), vmem(2, 2, 32, cols),
            vmem(2, 4, 8, cols),
            vmem(8, cols), vmem(ngx - 1, 8, cols), vmem(8, cols), vmem(ngy - 1, 8, cols),
            pltpu.SemaphoreType.DMA((2, 4)), pltpu.SemaphoreType.DMA((2, 4)),
            pltpu.SemaphoreType.DMA((ngx - 1,)), pltpu.SemaphoreType.DMA((ngx - 1,)),
            pltpu.SemaphoreType.DMA((ngy - 1,)), pltpu.SemaphoreType.DMA((ngy - 1,)),
        ],
        compiler_params=pltpu.CompilerParams(collective_id=0, has_side_effects=True,
                                             vmem_limit_bytes=32 * 1024 * 1024),
        name="dg_two_sections",
    )(state.reshape(flat))
    return tuple(o.reshape(shape) for o in out)


def solution(mesh):
    spec = P(None, None, None, "gy", "gx")
    return jax.shard_map(
        functools.partial(local, mesh.shape["gx"], mesh.shape["gy"]),
        mesh=mesh,
        in_specs=(spec,),
        out_specs=(spec, spec),
        check_vma=False,
    )
```

time: 166 us -> 27 us (0.16); the launches traced: 163 us -> 26.8 us
  other arithmetic: 64.8 us -> 0 us
  blocking collectives: 40 us -> 0 us
  local copies, waits for them, and re-layouts: 41.6 us -> 2.92 us
  Pallas kernels: 0 us -> 23.2 us
  starting transfers between devices: 11 us -> 0 us
  between operations: 3.75 us -> 0.65 us
  matrix products: 2.28 us -> 0 us
    pmax x1 -> x0, blocking collectives: 40 us -> none  [local(): global_top = lax.pmax(local_top, ('gx', 'gy'))]
    mul x40 -> x0, other arithmetic: 26 us -> none  [the longest x10 11 us: two_point(): mass_flux * mean_first + (mean_pressure if normal_dir == 0 else 0.0)]
    add x19 -> x0, other arithmetic: 24.8 us -> none  [the longest x8 7.79 us: two_point(): mass_flux * mean_second + (mean_pressure if normal_dir == 1 else 0.0)]
    pallas_call x0 -> x1, Pallas kernels: none -> 23.2 us  [local(): pl.pallas_call(functools.partial(kernel, ngx, ngy), out_shape=(jax.ShapeD...]
    ppermute x8 -> x0, starting transfers between devices: 11 us -> none  [the longest x4 10.5 us: with_halo(): lax.ppermute(head, axis, [((i + 1) % count, i) for i in range(count)])]
    unnamed x384 -> x4, local copies, waits for them, and re-layouts: 13.6 us -> 2.92 us
    another operation x17 -> x0, local copies, waits for them, and re-layouts: 9.33 us -> none  [the longest x2 1.65 us: section_rate(): column_got[3, :20].reshape(4, 5, rows)[:, :, None, :, None]]
    slice x18 -> x0, local copies, waits for them, and re-layouts: 7.05 us -> none  [the longest x2 1.71 us: section_rate(): current[:, 4, :, -1, :].reshape(20, cols)]
  transfers between devices with their start and end apart: 8 -> 0, of which waited for: 0 -> 0; matrix products, arithmetic and copies ran while one was open for 33% -> 0% of each run, Pallas kernels for 0% -> 0%
where the time goes in v1:
time: 27 us; the launch traced here: 26.8 us
  Pallas kernels  23.2 us (86%)
  local copies, waits for them, and re-layouts  2.92 us (11%)
  between operations  0.65 us (2%)
    pallas_call x1, Pallas kernels, local(): pl.pallas_call(functools.partial(kernel, ngx, ngy), out_shape=(jax.ShapeD...  23.2 us
    unnamed x4, local copies, waits for them, and re-layouts  2.92 us

profile of v1, /device:TPU:0, one launch (start us, length us, event | category | flops | bytes accessed | tf_op | source)
XLA Modules:
  0.0 26.8 jit_solution(7258614718987520613)
XLA Ops:
  0.6 0.0 copy-start
  0.6 1.1 %copy-done = f32[4,5,5,16,128]{4,3,2,1,0:T(8,128)S(1)} copy-done((f32[4,5,5,16,128]{4,3,2,1,0:T(8,128)S(1)}, f32[4,5,5,16,128]{4,3,2,1,0:T(8,128)}, u32[]{:S(2)}) %copy-start) | copy-done | bytes 819224
  1.8 23.2 %dg_two_sections.1 = (f32[4,25,16,128]{3,2,1,0:T(8,128)S(1)}, f32[4,25,16,128]{3,2,1,0:T(8,128)S(1)}) custom-call(f32[4,25,16,128]{3,2,1,0:T(8,128)S(1)} %bitcast.3), custom_call_target="tpu_custom_call" | custom-call | tf_op jit(solution)/shard_map/dg_two_sections/pallas_call | solution.py:426
  25.0 0.9 %copy.5 = f32[4,5,5,16,128]{4,3,2,1,0:T(8,128)} copy(f32[4,5,5,16,128]{4,3,2,1,0:T(8,128)S(1)} %bitcast.5) | data formatting | bytes 1638400
  25.9 0.9 %copy.6 = f32[4,5,5,16,128]{4,3,2,1,0:T(8,128)} copy(f32[4,5,5,16,128]{4,3,2,1,0:T(8,128)S(1)} %bitcast.4) | data formatting | bytes 1638400
Async XLA Ops:
  0.6 1.1 %copy-start = (f32[4,5,5,16,128]{4,3,2,1,0:T(8,128)S(1)}, f32[4,5,5,16,128]{4,3,2,1,0:T(8,128)}, u32[]{:S(2)}) copy-start(f32[4,5,5,16,128]{4,3,2,1,0:T(8,128)} %param.1) | copy-start | bytes 2457604

commit v2 on v1

--- a/solution.py
+++ b/solution.py
@@ -14,6 +14,8 @@
 F32 = jnp.float32
 LANES = 128
 RHO, HX, HY, PR, LR, BE, LB, HC = range(8)
+NEAR = 1.0 / 64.0
+ENERGY = [1.0, 1.0, 1.0, 2.0]
 
 
 def tables():
@@ -40,39 +42,32 @@
 WINV = [float(1.0 / w) for w in WEIGHTS]
 
 
-def coarse_inv(x):
+def inv(x):
     return pl.reciprocal(x, approx=True)
 
 
-def inv(x):
-    r = pl.reciprocal(x, approx=True)
-    return r * (2.0 - x * r)
-
-
-def series(f):
-    return 2.0 + f * (2.0 / 3.0 + f * (2.0 / 5.0 + f * (2.0 / 7.0 + f * (2.0 / 9.0))))
-
-
-def pair_flux(l, r, n):
-    d = r[RHO] - l[RHO]
-    s = r[RHO] + l[RHO]
-    z = d * coarse_inv(s)
-    f = z * z
-    near = f < 0.03
-    mean_rho = jnp.where(near, s, d) * inv(jnp.where(near, series(f), r[LR] - l[LR]))
-    d2 = r[BE] - l[BE]
-    s2 = r[BE] + l[BE]
-    z2 = d2 * coarse_inv(s2)
-    f2 = z2 * z2
-    near2 = f2 < 0.03
-    thermal = jnp.where(near2, series(f2), r[LB] - l[LB]) * inv(jnp.where(near2, s2, d2))
+def pair_flux(l, r, n, q=None):
+    gap = r[LR] - l[LR]
+    square = gap * gap
+    even = (r[RHO] + l[RHO]) * (0.5 + square * (-1.0 / 24.0 + square * (1.0 / 240.0)))
+    mean_rho = jnp.where(square < NEAR, even, (r[RHO] - l[RHO]) * inv(gap))
+    gap2 = r[LB] - l[LB]
+    square2 = gap2 * gap2
+    near = square2 < NEAR * 1.25 * 1.25
+    c1, c2 = 2.5 / 12.0 / 1.25**2, -2.5 / 720.0 / 1.25**4
+    top = jnp.where(near, 2.5 + square2 * (c1 + square2 * c2), gap2)
+    thermal = top * inv(jnp.where(near, r[BE] + l[BE], r[BE] - l[BE]))
     hn, ht = (HX, HY) if n == 0 else (HY, HX)
-    mass = mean_rho * (l[hn] + r[hn])
-    normal = mass * (l[hn] + r[hn]) + 0.5 * (l[PR] + r[PR])
+    along = l[hn] + r[hn]
+    mass = mean_rho * along
+    push = l[PR] + r[PR]
+    work = l[PR] * r[hn] + r[PR] * l[hn]
+    dot = l[HX] * r[HX] + l[HY] * r[HY]
+    if q is not None:
+        mass, push, work = q * mass, q * push, q * work
+    normal = mass * along + push
     tangent = mass * (l[ht] + r[ht])
-    energy = mass * (2.0 * (l[HX] * r[HX] + l[HY] * r[HY]) + 2.5 * thermal) + (
-        l[PR] * r[hn] + r[PR] * l[hn]
-    )
+    energy = mass * (dot + thermal) + work
     return (mass, normal, tangent, energy) if n == 0 else (mass, tangent, normal, energy)
 
 
@@ -84,8 +79,8 @@
     beta = u[0] * inv(pressure)
     half_sound = jnp.sqrt(0.35 * pressure * ri)
     log_rho = jnp.log(u[0])
-    log_beta = log_rho - jnp.log(pressure)
-    return (u[0], 0.5 * vx, 0.5 * vy, pressure, log_rho, beta, log_beta, half_sound)
+    log_beta = 1.25 * (log_rho - jnp.log(pressure))
+    return (u[0], 0.5 * vx, 0.5 * vy, 0.5 * pressure, log_rho, beta, log_beta, half_sound)
 
 
 def face_of(l, r, el, er, n):
@@ -97,7 +92,7 @@
         flux[0] - fast * (r[RHO] - l[RHO]),
         flux[1] - fast2 * (r[RHO] * r[HX] - l[RHO] * l[HX]),
         flux[2] - fast2 * (r[RHO] * r[HY] - l[RHO] * l[HY]),
-        flux[3] - fast * (er - el),
+        flux[3] + flux[3] - fast * (er - el),
     )
 
 
@@ -114,12 +109,101 @@
     return out
 
 
+def tile(h):
+    return pl.ds(pl.multiple_of(h * 8, 8), 8)
+
+
+def line_terms(prim, n, node, r, u):
+    def load(k):
+        return [prim[q, node(k), r, :] for q in range(7)]
+
+    acc = [[None] * 4 for _ in range(5)]
+    for i in range(5):
+        for j in range(i + 1, 5):
+            q = float(2.0 * WEIGHTS[i] * DERIV[i, j])
+            flux = pair_flux(load(i), load(j), n, q)
+            for v in range(4):
+                term = flux[v]
+                acc[i][v] = term if acc[i][v] is None else acc[i][v] + term
+                acc[j][v] = -term if acc[j][v] is None else acc[j][v] - term
+    hn = HX if n == 0 else HY
+
+    def half(k):
+        c = [u[v, node(k), r, :] for v in range(4)]
+        speed = prim[hn, node(k), r, :]
+        p = prim[PR, node(k), r, :]
+        h = [0.5 * c[1 + n], speed * c[1], speed * c[2], speed * (0.5 * c[3] + p)]
+        h[1 + n] = h[1 + n] + p
+        return c, h, jnp.abs(speed) + prim[HC, node(k), r, :]
+
+    before = half(0)
+    prev = None
+    outs = []
+    for k in range(5):
+        if k < 4:
+            after = half(k + 1)
+            fast = jnp.maximum(before[2], after[2])
+            g = [
+                before[1][v] + after[1][v]
+                - (fast if v < 3 else 0.5 * fast) * (after[0][v] - before[0][v])
+                for v in range(4)
+            ]
+            before = after
+        for v in range(4):
+            if k == 0:
+                t = g[v]
+            elif k == 4:
+                t = -prev[v]
+            else:
+                t = g[v] - prev[v]
+            w = WINV[k] * ENERGY[v]
+            outs.append((k, v, acc[k][v] * -w, (acc[k][v] - t) * w))
+        prev = g
+    return outs
+
+
+def column_y(i, prim, rx, sx, fy, blend, u, sink):
+    def inner(h, c):
+        r = tile(h)
+        share = blend[r, :]
+        for k, v, vol, diff in line_terms(prim, 1, lambda k: k * 5 + i, r, u):
+            m = k * 5 + i
+            rate = (rx[v, m, r, :] + vol) + share * (sx[v, m, r, :] + diff)
+            if k == 0:
+                rate = rate + WINV[0] * fy[i, 0, v, r, :]
+            if k == 4:
+                rate = rate - WINV[4] * fy[i, 1, v, r, :]
+            sink(v, k, m, r, rate)
+        return c
+
+    lax.fori_loop(0, blend.shape[0] // 8, inner, 0)
+
+
+def volume_y(prim, rx, sx, fy, blend, u, out):
+    def body(i, carry):
+        def sink(v, k, m, r, rate):
+            out[v, m, r, :] = rate
+
+        column_y(i, prim, rx, sx, fy, blend, u, sink)
+        return carry
+
+    lax.fori_loop(0, 5, body, 0)
+
+
 def kernel(
-    ngx, ngy, state, adv, tend,
-    prim, first, rx, sx, fx, fy, raw, blend, packx, packy, gotx, goty,
+    ngx, ngy, state_hbm, state, prim, first, rx, sx, fy, blend, step_ref,
+    rate, fx, raw, packx, packy, gotx, goty,
     edge, top, top_got, top2, top2_got,
-    hs, hr, ts, tr, t2s, t2r,
+    ins, hs, hr, ts, tr, t2s, t2r,
 ):
+    loads = [
+        pltpu.make_async_copy(
+            state_hbm.at[:, pl.ds(a * 5, 5)], state.at[:, pl.ds(a * 5, 5)], ins.at[a]
+        )
+        for a in range(5)
+    ]
+    for copy in loads:
+        copy.start()
     gx = lax.axis_index("gx")
     gy = lax.axis_index("gy")
     at_x = lambda d: (lax.rem(gx + d, ngx), gy)
@@ -135,9 +219,6 @@
 
     lane = lax.broadcasted_iota(jnp.int32, (rows, LANES), 1)
     row = lax.broadcasted_iota(jnp.int32, (rows, LANES), 0)
-
-    def tile(h):
-        return pl.ds(pl.multiple_of(h * 8, 8), 8)
 
     def remote(src, dst, send, recv, device):
         return pltpu.make_async_remote_copy(
@@ -222,57 +303,11 @@
 
         lax.fori_loop(0, 5, body, 0)
 
-    def line_terms(n, node, r, u):
-        def load(k):
-            return [prim[q, node(k), r, :] for q in range(7)]
-
-        acc = [[None] * 4 for _ in range(5)]
-        for i in range(5):
-            for j in range(i + 1, 5):
-                q = float(2.0 * WEIGHTS[i] * DERIV[i, j])
-                flux = pair_flux(load(i), load(j), n)
-                for v in range(4):
-                    term = q * flux[v]
-                    acc[i][v] = term if acc[i][v] is None else acc[i][v] + term
-                    acc[j][v] = -term if acc[j][v] is None else acc[j][v] - term
-        hn = HX if n == 0 else HY
-
-        def half(k):
-            c = [u[v, node(k), r, :] for v in range(4)]
-            speed = prim[hn, node(k), r, :]
-            p = prim[PR, node(k), r, :]
-            h = [0.5 * c[1 + n], speed * c[1], speed * c[2], speed * (c[3] + p)]
-            h[1 + n] = h[1 + n] + 0.5 * p
-            return c, h, jnp.abs(speed) + prim[HC, node(k), r, :]
-
-        before = half(0)
-        prev = None
-        outs = []
-        for k in range(5):
-            if k < 4:
-                after = half(k + 1)
-                fast = jnp.maximum(before[2], after[2])
-                g = [
-                    before[1][v] + after[1][v] - fast * (after[0][v] - before[0][v])
-                    for v in range(4)
-                ]
-                before = after
-            for v in range(4):
-                if k == 0:
-                    t = g[v]
-                elif k == 4:
-                    t = -prev[v]
-                else:
-                    t = g[v] - prev[v]
-                outs.append((k, v, acc[k][v] * -WINV[k], (acc[k][v] - t) * WINV[k]))
-            prev = g
-        return outs
-
     def volume_x(u):
         def body(i, carry):
             def inner(h, c):
                 r = tile(h)
-                for k, v, vol, diff in line_terms(0, lambda k: i * 5 + k, r, u):
+                for k, v, vol, diff in line_terms(prim, 0, lambda k: i * 5 + k, r, u):
                     rx[v, i * 5 + k, r, :] = vol
                     sx[v, i * 5 + k, r, :] = diff
                 return c
@@ -319,33 +354,22 @@
         beside = jnp.maximum(jnp.maximum(left, right), jnp.maximum(below, above))
         blend[...] = jnp.maximum(own, 0.5 * beside)
 
-    def volume_y(u, sink):
-        def body(i, carry):
-            def inner(h, c):
-                r = tile(h)
-                share = blend[r, :]
-                for k, v, vol, diff in line_terms(1, lambda k: k * 5 + i, r, u):
-                    m = k * 5 + i
-                    rate = (rx[v, m, r, :] + vol) + share * (sx[v, m, r, :] + diff)
-                    if k == 0:
-                        rate = rate + WINV[0] * fy[i, 0, v, r, :]
-                    if k == 4:
-                        rate = rate - WINV[4] * fy[i, 1, v, r, :]
-                    sink(v, m, r, rate)
-                return c
-
-            return lax.fori_loop(0, halves, inner, carry)
-
-        lax.fori_loop(0, 5, body, 0)
-
-    def prepare(m, fastest):
-        q = primitives_of([state[v, m] for v in range(4)])
-        for f in range(8):
-            prim[f, m] = q[f]
-        speed = jnp.sqrt(q[HX] * q[HX] + q[HY] * q[HY]) + q[HC]
-        return jnp.maximum(fastest, speed)
-
-    fastest = lax.fori_loop(0, 25, prepare, jnp.zeros((rows, LANES), F32))
+    def prepare(a, fastest):
+        for m in [a * 5 + b for b in range(5)]:
+            q = primitives_of([state[v, m] for v in range(4)])
+            for f in range(8):
+                prim[f, m] = q[f]
+            speed = jnp.sqrt(q[HX] * q[HX] + q[HY] * q[HY]) + q[HC]
+            fastest = jnp.maximum(fastest, speed)
+        return fastest
+
+    def load_and_prepare(a, fastest):
+        pltpu.make_async_copy(
+            state_hbm.at[:, pl.ds(a * 5, 5)], state.at[:, pl.ds(a * 5, 5)], ins.at[a]
+        ).wait()
+        return prepare(a, fastest)
+
+    fastest = lax.fori_loop(0, 5, load_and_prepare, jnp.zeros((rows, LANES), F32))
     local_top = fastest[0:8]
     for h in range(1, halves):
         local_top = jnp.maximum(local_top, fastest[8 * h : 8 * h + 8])
@@ -360,13 +384,13 @@
     for copy in halos + tops:
         copy.start()
     faces(state)
+    volume_x(state)
     for copy in tops:
         copy.wait()
     local_top = top[...]
     for d in range(ngx - 1):
         local_top = jnp.maximum(local_top, top_got[d])
     top2[...] = local_top
-    volume_x(state)
     tops = [
         remote(top2, top2_got.at[d - 1], t2s.at[d - 1], t2r.at[d - 1], at_y(d))
         for d in range(1, ngy)
@@ -377,10 +401,7 @@
         copy.wait()
     finish_halo(0)
 
-    def keep_rate(v, m, r, rate):
-        tend[v, m, r, :] = rate
-
-    volume_y(state, keep_rate)
+    volume_y(prim, rx, sx, fy, blend, state, rate)
     for copy in tops:
         copy.wait()
     local_top = top2[...]
@@ -390,32 +411,56 @@
     step = jnp.broadcast_to(step, (8, LANES))
     step_full = jnp.concatenate([step] * halves, axis=0)
 
-    def prepare2(m, carry):
-        u = [state[v, m] + step_full * tend[v, m] for v in range(4)]
-        for v in range(4):
-            first[v, m] = u[v]
-        q = primitives_of(u)
-        for f in range(8):
-            prim[f, m] = q[f]
+    def prepare2(a, carry):
+        for m in [a * 5 + b for b in range(5)]:
+            u = [state[v, m] + step_full * rate[v, m] for v in range(4)]
+            for v in range(4):
+                first[v, m] = u[v]
+            q = primitives_of(u)
+            for f in range(8):
+                prim[f, m] = q[f]
         return carry
 
-    lax.fori_loop(0, 25, prepare2, 0)
+    lax.fori_loop(0, 5, prepare2, 0)
     indicator(1)
     pack(1, first)
-    faces(first)
     halos = halo_copies(1)
     for copy in halos:
         copy.start()
+    step_ref[...] = step
+    faces(first)
     volume_x(first)
     for copy in halos:
         copy.wait()
     finish_halo(1)
 
-    def keep_both(v, m, r, rate):
-        tend[v, m, r, :] = rate
-        adv[v, m, r, :] = 0.5 * state[v, m, r, :] + 0.5 * (first[v, m, r, :] + step * rate)
-
-    volume_y(first, keep_both)
+
+def last_kernel(state, prim, first, rx, sx, fy, blend, step_ref, adv, tend, adv_v, tend_v, sems):
+    step = step_ref[...]
+
+    def column(i):
+        pairs = ((adv_v, adv), (tend_v, tend))
+        return [
+            pltpu.make_async_copy(src.at[i], dst.at[:, :, i], sems.at[k, i])
+            for k, (src, dst) in enumerate(pairs)
+        ]
+
+    def body(i, carry):
+        def sink(v, k, m, r, rate):
+            tend_v[i, v, k, r, :] = rate
+            adv_v[i, v, k, r, :] = 0.5 * state[v, m, r, :] + 0.5 * (
+                first[v, m, r, :] + step * rate
+            )
+
+        column_y(i, prim, rx, sx, fy, blend, first, sink)
+        for copy in column(i):
+            copy.start()
+        return carry
+
+    lax.fori_loop(0, 5, body, 0)
+    for i in range(5):
+        for copy in column(i):
+            copy.wait()
 
 
 def local(ngx, ngy, state):
@@ -423,29 +468,40 @@
     rows, cols = shape[3], shape[4]
     flat = (4, 25, rows, cols)
     vmem = lambda *s: pltpu.VMEM(s, F32)
-    out = pl.pallas_call(
+    whole = pl.BlockSpec(memory_space=pltpu.VMEM)
+    hbm = pl.BlockSpec(memory_space=pltpu.HBM)
+    mid = [flat, (8, 25, rows, cols), flat, flat, flat, (5, 2, 4, rows, cols), (rows, cols), (8, cols)]
+    kept = pl.pallas_call(
         functools.partial(kernel, ngx, ngy),
-        out_shape=(jax.ShapeDtypeStruct(flat, F32),) * 2,
-        in_specs=[pl.BlockSpec(memory_space=pltpu.VMEM)],
-        out_specs=[pl.BlockSpec(memory_space=pltpu.VMEM)] * 2,
+        out_shape=[jax.ShapeDtypeStruct(m, F32) for m in mid],
+        in_specs=[hbm],
+        out_specs=[whole] * len(mid),
         scratch_shapes=[
-            vmem(8, 25, rows, cols),
-            vmem(*flat), vmem(*flat), vmem(*flat),
-            vmem(5, 2, 4, rows, cols), vmem(5, 2, 4, rows, cols),
-            vmem(rows, cols), vmem(rows, cols),
+            vmem(*flat), vmem(5, 2, 4, rows, cols), vmem(rows, cols),
             vmem(2, 2, rows, cols), vmem(2, 2, 32, cols),
             vmem(2, 2, rows, cols), vmem(2, 2, 32, cols),
             vmem(2, 4, 8, cols),
             vmem(8, cols), vmem(ngx - 1, 8, cols), vmem(8, cols), vmem(ngy - 1, 8, cols),
+            pltpu.SemaphoreType.DMA((5,)),
             pltpu.SemaphoreType.DMA((2, 4)), pltpu.SemaphoreType.DMA((2, 4)),
             pltpu.SemaphoreType.DMA((ngx - 1,)), pltpu.SemaphoreType.DMA((ngx - 1,)),
             pltpu.SemaphoreType.DMA((ngy - 1,)), pltpu.SemaphoreType.DMA((ngy - 1,)),
         ],
         compiler_params=pltpu.CompilerParams(collective_id=0, has_side_effects=True,
-                                             vmem_limit_bytes=32 * 1024 * 1024),
-        name="dg_two_sections",
-    )(state.reshape(flat))
-    return tuple(o.reshape(shape) for o in out)
+                                             vmem_limit_bytes=16 * 1024 * 1024),
+        name="dg_sections",
+    )(pltpu.with_memory_space_constraint(state.reshape(flat), pltpu.HBM))
+    return pl.pallas_call(
+        last_kernel,
+        out_shape=(jax.ShapeDtypeStruct(shape, F32),) * 2,
+        in_specs=[whole] * len(mid),
+        out_specs=[hbm] * 2,
+        scratch_shapes=[
+            vmem(5, 4, 5, rows, cols), vmem(5, 4, 5, rows, cols), pltpu.SemaphoreType.DMA((2, 5))
+        ],
+        compiler_params=pltpu.CompilerParams(vmem_limit_bytes=16 * 1024 * 1024),
+        name="dg_last_pass",
+    )(*kept)
 
 
 def solution(mesh):

time: 27 us -> 21.8 us (0.81)
  local copies, waits for them, and re-layouts: 2.92 us -> 0 us
  Pallas kernels: 23.2 us -> 21 us
    unnamed x4 -> x0, local copies, waits for them, and re-layouts: 2.92 us -> none
    pallas_call x1 -> x2, Pallas kernels: 23.2 us -> 21 us  [the longest x1 18.8 us: local(): pl.pallas_call(functools.partial(kernel, ngx, ngy), out_shape=[jax.ShapeD...]
where the time goes in v2:
time: 21.8 us; the launch traced here: 21.6 us
  Pallas kernels  21 us (96%)
  between operations  0.64 us (3%)
    pallas_call x1, Pallas kernels, local(): pl.pallas_call(functools.partial(kernel, ngx, ngy), out_shape=[jax.ShapeD...  18.8 us
    pallas_call x1, Pallas kernels, local(): pl.pallas_call(last_kernel, out_shape=(jax.ShapeDtypeStruct(shape, F32),)...  2.18 us

profile of v2, /device:TPU:0, one launch (start us, length us, event | category | flops | bytes accessed | tf_op | source)
XLA Modules:
  0.0 21.6 jit_solution(13569361274325840468)
XLA Ops:
  0.6 18.8 %dg_sections.1 = (f32[4,25,16,128]{3,2,1,0:T(8,128)S(1)}, f32[8,25,16,128]{3,2,1,0:T(8,128)S(1)}, f32[4,25,16,128]{3,2,1,0:T(8,128)S(1)}, f32[4,25,16,128]{3,2,1...) custom-call(f32[4,25,16,128]{3,2,1,0:T(8,128)} %bitcast.1), custom_call_target="tpu_custom_call" | custom-call | tf_op jit(solution)/shard_map/dg_sections/pallas_call | solution.py:474
  19.4 2.2 %dg_last_pass.1 = (f32[4,5,5,16,128]{4,3,2,1,0:T(8,128)}, f32[4,5,5,16,128]{4,3,2,1,0:T(8,128)}) custom-call(f32[4,25,16,128]{3,2,1,0:T(8,128)S(1)} %get-tuple-element.10.state, f32[8,25,16,128]{3,2,1,0:T(8,128)S(1)} %get-tuple-element.11.prim, f32[4,25,16,128]{3,2,1,0:T(8,128)S(1)} %get-tuple-element.12.first, f32[4,25,16,128]{3,2,1,0:T(8,128)S(1)} %get-tuple-element.13.rx, ...), custom_call_target="tpu_custom_call" | custom-call | tf_op jit(solution)/shard_map/dg_last_pass/pallas_call | solution.py:494

commit v3 on v2

--- a/solution.py
+++ b/solution.py
@@ -15,6 +15,7 @@
 LANES = 128
 RHO, HX, HY, PR, LR, BE, LB, HC = range(8)
 NEAR = 1.0 / 64.0
+EARLY = 2
 ENERGY = [1.0, 1.0, 1.0, 2.0]
 
 
@@ -162,6 +163,24 @@
     return outs
 
 
+def finished_column(i, rx, sx, fy, blend, sink):
+    def inner(h, c):
+        r = tile(h)
+        share = blend[r, :]
+        for k in range(5):
+            m = k * 5 + i
+            for v in range(4):
+                rate = rx[v, m, r, :] + share * sx[v, m, r, :]
+                if k == 0:
+                    rate = rate + WINV[0] * fy[i, 0, v, r, :]
+                if k == 4:
+                    rate = rate - WINV[4] * fy[i, 1, v, r, :]
+                sink(v, k, m, r, rate)
+        return c
+
+    lax.fori_loop(0, blend.shape[0] // 8, inner, 0)
+
+
 def column_y(i, prim, rx, sx, fy, blend, u, sink):
     def inner(h, c):
         r = tile(h)
@@ -192,9 +211,9 @@
 
 def kernel(
     ngx, ngy, state_hbm, state, prim, first, rx, sx, fy, blend, step_ref,
-    rate, fx, raw, packx, packy, gotx, goty,
-    edge, top, top_got, top2, top2_got,
-    ins, hs, hr, ts, tr, t2s, t2r,
+    rate, product, fx, raw, packx, packy, gotx, goty,
+    edge, top, top_got,
+    ins, hs, hr, ts, tr,
 ):
     loads = [
         pltpu.make_async_copy(
@@ -212,10 +231,11 @@
     halves = rows // 8
 
     barrier = pltpu.get_barrier_semaphore()
-    for d in range(1, ngx):
-        pl.semaphore_signal(barrier, inc=1, device_id=at_x(d), device_id_type=MESH)
-    for d in range(1, ngy):
-        pl.semaphore_signal(barrier, inc=1, device_id=at_y(d), device_id_type=MESH)
+    peers = [
+        (lax.rem(gx + d // ngy, ngx), lax.rem(gy + d % ngy, ngy)) for d in range(1, ngx * ngy)
+    ]
+    for peer in peers:
+        pl.semaphore_signal(barrier, inc=1, device_id=peer, device_id_type=MESH)
 
     lane = lax.broadcasted_iota(jnp.int32, (rows, LANES), 1)
     row = lax.broadcasted_iota(jnp.int32, (rows, LANES), 0)
@@ -241,7 +261,7 @@
             for a in range(5):
                 lines.append(
                     transform(
-                        [prim[RHO, a * 5 + b, r, :] * prim[PR, a * 5 + b, r, :] for b in range(5)]
+                        [product[a * 5 + b, r, :] for b in range(5)]
                     )
                 )
             sums = {}
@@ -354,11 +374,23 @@
         beside = jnp.maximum(jnp.maximum(left, right), jnp.maximum(below, above))
         blend[...] = jnp.maximum(own, 0.5 * beside)
 
+    def early_column(i, carry):
+        def inner(h, c):
+            r = tile(h)
+            for k, v, vol, diff in line_terms(prim, 1, lambda k: k * 5 + i, r, first):
+                m = k * 5 + i
+                rx[v, m, r, :] = rx[v, m, r, :] + vol
+                sx[v, m, r, :] = sx[v, m, r, :] + diff
+            return c
+
+        return lax.fori_loop(0, halves, inner, carry)
+
     def prepare(a, fastest):
         for m in [a * 5 + b for b in range(5)]:
             q = primitives_of([state[v, m] for v in range(4)])
             for f in range(8):
                 prim[f, m] = q[f]
+            product[m] = q[RHO] * q[PR]
             speed = jnp.sqrt(q[HX] * q[HX] + q[HY] * q[HY]) + q[HC]
             fastest = jnp.maximum(fastest, speed)
         return fastest
@@ -373,63 +405,61 @@
     local_top = fastest[0:8]
     for h in range(1, halves):
         local_top = jnp.maximum(local_top, fastest[8 * h : 8 * h + 8])
-    top[...] = local_top
+    top[...] = jnp.broadcast_to(jnp.max(local_top, axis=0, keepdims=True), (8, LANES))
     indicator(0)
     pack(0, state)
-    pl.semaphore_wait(barrier, ngx + ngy - 2)
+    pl.semaphore_wait(barrier, ngx * ngy - 1)
+    for d, peer in enumerate(peers):
+        remote(
+            top.at[pl.ds(0, 1)], top_got.at[d, pl.ds(0, 1)], ts.at[0], tr.at[0], peer
+        ).start()
     halos = halo_copies(0)
-    tops = [
-        remote(top, top_got.at[d - 1], ts.at[d - 1], tr.at[d - 1], at_x(d)) for d in range(1, ngx)
-    ]
-    for copy in halos + tops:
+    for copy in halos:
         copy.start()
     faces(state)
     volume_x(state)
-    for copy in tops:
-        copy.wait()
-    local_top = top[...]
-    for d in range(ngx - 1):
-        local_top = jnp.maximum(local_top, top_got[d])
-    top2[...] = local_top
-    tops = [
-        remote(top2, top2_got.at[d - 1], t2s.at[d - 1], t2r.at[d - 1], at_y(d))
-        for d in range(1, ngy)
-    ]
-    for copy in tops:
-        copy.start()
     for copy in halos:
         copy.wait()
     finish_halo(0)
-
     volume_y(prim, rx, sx, fy, blend, state, rate)
-    for copy in tops:
-        copy.wait()
-    local_top = top2[...]
-    for d in range(ngy - 1):
-        local_top = jnp.maximum(local_top, top2_got[d])
-    step = (COURANT * 2.0 / 9.0) / (2.0 * jnp.max(local_top, keepdims=True))
+    every = top_got.at[:, pl.ds(0, 1)]
+    tops = remote(every, every, ts.at[0], tr.at[0], peers[0])
+    tops.wait_recv()
+    best = top[0:1, :]
+    for d in range(len(peers)):
+        best = jnp.maximum(best, top_got[d, 0:1, :])
+    step = (COURANT * 2.0 / 9.0) / (2.0 * jnp.max(best, axis=1, keepdims=True))
     step = jnp.broadcast_to(step, (8, LANES))
     step_full = jnp.concatenate([step] * halves, axis=0)
 
-    def prepare2(a, carry):
+    def advance(a, carry):
         for m in [a * 5 + b for b in range(5)]:
             u = [state[v, m] + step_full * rate[v, m] for v in range(4)]
             for v in range(4):
                 first[v, m] = u[v]
-            q = primitives_of(u)
-            for f in range(8):
-                prim[f, m] = q[f]
+            product[m] = u[0] * u[3] - 0.5 * (u[1] * u[1] + u[2] * u[2])
         return carry
 
-    lax.fori_loop(0, 5, prepare2, 0)
+    lax.fori_loop(0, 5, advance, 0)
     indicator(1)
     pack(1, first)
     halos = halo_copies(1)
     for copy in halos:
         copy.start()
     step_ref[...] = step
+
+    def prepare2(a, carry):
+        for m in [a * 5 + b for b in range(5)]:
+            q = primitives_of([first[v, m] for v in range(4)])
+            for f in range(8):
+                prim[f, m] = q[f]
+        return carry
+
+    lax.fori_loop(0, 5, prepare2, 0)
     faces(first)
     volume_x(first)
+    lax.fori_loop(0, EARLY, early_column, 0)
+    tops.wait_send()
     for copy in halos:
         copy.wait()
     finish_halo(1)
@@ -445,19 +475,23 @@
             for k, (src, dst) in enumerate(pairs)
         ]
 
-    def body(i, carry):
+    def body(early, i, carry):
         def sink(v, k, m, r, rate):
             tend_v[i, v, k, r, :] = rate
             adv_v[i, v, k, r, :] = 0.5 * state[v, m, r, :] + 0.5 * (
                 first[v, m, r, :] + step * rate
             )
 
-        column_y(i, prim, rx, sx, fy, blend, first, sink)
+        if early:
+            finished_column(i, rx, sx, fy, blend, sink)
+        else:
+            column_y(i, prim, rx, sx, fy, blend, first, sink)
         for copy in column(i):
             copy.start()
         return carry
 
-    lax.fori_loop(0, 5, body, 0)
+    lax.fori_loop(0, EARLY, functools.partial(body, True), 0)
+    lax.fori_loop(EARLY, 5, functools.partial(body, False), 0)
     for i in range(5):
         for copy in column(i):
             copy.wait()
@@ -477,15 +511,14 @@
         in_specs=[hbm],
         out_specs=[whole] * len(mid),
         scratch_shapes=[
-            vmem(*flat), vmem(5, 2, 4, rows, cols), vmem(rows, cols),
+            vmem(*flat), vmem(25, rows, cols), vmem(5, 2, 4, rows, cols), vmem(rows, cols),
             vmem(2, 2, rows, cols), vmem(2, 2, 32, cols),
             vmem(2, 2, rows, cols), vmem(2, 2, 32, cols),
             vmem(2, 4, 8, cols),
-            vmem(8, cols), vmem(ngx - 1, 8, cols), vmem(8, cols), vmem(ngy - 1, 8, cols),
+            vmem(8, cols), vmem(ngx * ngy - 1, 8, cols),
             pltpu.SemaphoreType.DMA((5,)),
             pltpu.SemaphoreType.DMA((2, 4)), pltpu.SemaphoreType.DMA((2, 4)),
-            pltpu.SemaphoreType.DMA((ngx - 1,)), pltpu.SemaphoreType.DMA((ngx - 1,)),
-            pltpu.SemaphoreType.DMA((ngy - 1,)), pltpu.SemaphoreType.DMA((ngy - 1,)),
+            pltpu.SemaphoreType.DMA((1,)), pltpu.SemaphoreType.DMA((1,)),
         ],
         compiler_params=pltpu.CompilerParams(collective_id=0, has_side_effects=True,
                                              vmem_limit_bytes=16 * 1024 * 1024),

time: 21.8 us -> 20.3 us (0.931)
  Pallas kernels: 21 us -> 19.5 us
    pallas_call x1, Pallas kernels: 18.8 us -> 17.7 us  [local(): pl.pallas_call(functools.partial(kernel, ngx, ngy), out_shape=[jax.ShapeD...]
    pallas_call x1, Pallas kernels: 2.18 us -> 1.76 us  [local(): pl.pallas_call(last_kernel, out_shape=(jax.ShapeDtypeStruct(shape, F32),)...]
where the time goes in v3:
time: 20.3 us; the launch traced here: 20.1 us
  Pallas kernels  19.5 us (96%)
  between operations  0.64 us (3%)
    pallas_call x1, Pallas kernels, local(): pl.pallas_call(functools.partial(kernel, ngx, ngy), out_shape=[jax.ShapeD...  17.7 us
    pallas_call x1, Pallas kernels, local(): pl.pallas_call(last_kernel, out_shape=(jax.ShapeDtypeStruct(shape, F32),)...  1.76 us

profile of v3, /device:TPU:0, one launch (start us, length us, event | category | flops | bytes accessed | tf_op | source)
XLA Modules:
  0.0 20.1 jit_solution(13926968534672499896)
XLA Ops:
  0.6 17.7 %dg_sections.1 = (f32[4,25,16,128]{3,2,1,0:T(8,128)S(1)}, f32[8,25,16,128]{3,2,1,0:T(8,128)S(1)}, f32[4,25,16,128]{3,2,1,0:T(8,128)S(1)}, f32[4,25,16,128]{3,2,1...) custom-call(f32[4,25,16,128]{3,2,1,0:T(8,128)} %bitcast.1), custom_call_target="tpu_custom_call" | custom-call | tf_op jit(solution)/shard_map/dg_sections/pallas_call | solution.py:508
  18.4 1.8 %dg_last_pass.1 = (f32[4,5,5,16,128]{4,3,2,1,0:T(8,128)}, f32[4,5,5,16,128]{4,3,2,1,0:T(8,128)}) custom-call(f32[4,25,16,128]{3,2,1,0:T(8,128)S(1)} %get-tuple-element.10.state, f32[8,25,16,128]{3,2,1,0:T(8,128)S(1)} %get-tuple-element.11.prim, f32[4,25,16,128]{3,2,1,0:T(8,128)S(1)} %get-tuple-element.12.first, f32[4,25,16,128]{3,2,1,0:T(8,128)S(1)} %get-tuple-element.13.rx, ...), custom_call_target="tpu_custom_call" | custom-call | tf_op jit(solution)/shard_map/dg_last_pass/pallas_call | solution.py:527

commit v4 on v3

--- a/solution.py
+++ b/solution.py
@@ -15,7 +15,7 @@
 LANES = 128
 RHO, HX, HY, PR, LR, BE, LB, HC = range(8)
 NEAR = 1.0 / 64.0
-EARLY = 2
+EARLY = 4
 ENERGY = [1.0, 1.0, 1.0, 2.0]
 
 
@@ -199,14 +199,18 @@
 
 
 def volume_y(prim, rx, sx, fy, blend, u, out):
-    def body(i, carry):
+    def body(early, i, carry):
         def sink(v, k, m, r, rate):
             out[v, m, r, :] = rate
 
-        column_y(i, prim, rx, sx, fy, blend, u, sink)
+        if early:
+            finished_column(i, rx, sx, fy, blend, sink)
+        else:
+            column_y(i, prim, rx, sx, fy, blend, u, sink)
         return carry
 
-    lax.fori_loop(0, 5, body, 0)
+    lax.fori_loop(0, EARLY, functools.partial(body, True), 0)
+    lax.fori_loop(EARLY, 5, functools.partial(body, False), 0)
 
 
 def kernel(
@@ -374,10 +378,10 @@
         beside = jnp.maximum(jnp.maximum(left, right), jnp.maximum(below, above))
         blend[...] = jnp.maximum(own, 0.5 * beside)
 
-    def early_column(i, carry):
+    def early_column(u, i, carry):
         def inner(h, c):
             r = tile(h)
-            for k, v, vol, diff in line_terms(prim, 1, lambda k: k * 5 + i, r, first):
+            for k, v, vol, diff in line_terms(prim, 1, lambda k: k * 5 + i, r, u):
                 m = k * 5 + i
                 rx[v, m, r, :] = rx[v, m, r, :] + vol
                 sx[v, m, r, :] = sx[v, m, r, :] + diff
@@ -418,6 +422,7 @@
         copy.start()
     faces(state)
     volume_x(state)
+    lax.fori_loop(0, EARLY, functools.partial(early_column, state), 0)
     for copy in halos:
         copy.wait()
     finish_halo(0)
@@ -458,7 +463,7 @@
     lax.fori_loop(0, 5, prepare2, 0)
     faces(first)
     volume_x(first)
-    lax.fori_loop(0, EARLY, early_column, 0)
+    lax.fori_loop(0, EARLY, functools.partial(early_column, first), 0)
     tops.wait_send()
     for copy in halos:
         copy.wait()

time: 20.3 us -> 19.1 us (0.941)
  Pallas kernels: 19.5 us -> 18.3 us
    pallas_call x1, Pallas kernels: 17.7 us -> 16.9 us  [local(): pl.pallas_call(functools.partial(kernel, ngx, ngy), out_shape=[jax.ShapeD...]
    pallas_call x1, Pallas kernels: 1.76 us -> 1.34 us  [local(): pl.pallas_call(last_kernel, out_shape=(jax.ShapeDtypeStruct(shape, F32),)...]
where the time goes in v4:
time: 19.1 us; the launch traced here: 18.9 us
  Pallas kernels  18.3 us (96%)
  between operations  0.64 us (3%)
    pallas_call x1, Pallas kernels, local(): pl.pallas_call(functools.partial(kernel, ngx, ngy), out_shape=[jax.ShapeD...  16.9 us
    pallas_call x1, Pallas kernels, local(): pl.pallas_call(last_kernel, out_shape=(jax.ShapeDtypeStruct(shape, F32),)...  1.34 us

profile of v4, /device:TPU:0, one launch (start us, length us, event | category | flops | bytes accessed | tf_op | source)
XLA Modules:
  0.0 18.9 jit_solution(6612449481142193536)
XLA Ops:
  0.6 16.9 %dg_sections.1 = (f32[4,25,16,128]{3,2,1,0:T(8,128)S(1)}, f32[8,25,16,128]{3,2,1,0:T(8,128)S(1)}, f32[4,25,16,128]{3,2,1,0:T(8,128)S(1)}, f32[4,25,16,128]{3,2,1...) custom-call(f32[4,25,16,128]{3,2,1,0:T(8,128)} %bitcast.1), custom_call_target="tpu_custom_call" | custom-call | tf_op jit(solution)/shard_map/dg_sections/pallas_call | solution.py:513
  17.6 1.3 %dg_last_pass.1 = (f32[4,5,5,16,128]{4,3,2,1,0:T(8,128)}, f32[4,5,5,16,128]{4,3,2,1,0:T(8,128)}) custom-call(f32[4,25,16,128]{3,2,1,0:T(8,128)S(1)} %get-tuple-element.10.state, f32[8,25,16,128]{3,2,1,0:T(8,128)S(1)} %get-tuple-element.11.prim, f32[4,25,16,128]{3,2,1,0:T(8,128)S(1)} %get-tuple-element.12.first, f32[4,25,16,128]{3,2,1,0:T(8,128)S(1)} %get-tuple-element.13.rx, ...), custom_call_target="tpu_custom_call" | custom-call | tf_op jit(solution)/shard_map/dg_last_pass/pallas_call | solution.py:532

commit v5 on v4

--- a/solution.py
+++ b/solution.py
@@ -15,7 +15,7 @@
 LANES = 128
 RHO, HX, HY, PR, LR, BE, LB, HC = range(8)
 NEAR = 1.0 / 64.0
-EARLY = 4
+EARLY = 5
 ENERGY = [1.0, 1.0, 1.0, 2.0]
 
 
@@ -413,13 +413,13 @@
     indicator(0)
     pack(0, state)
     pl.semaphore_wait(barrier, ngx * ngy - 1)
+    halos = halo_copies(0)
+    for copy in halos:
+        copy.start()
     for d, peer in enumerate(peers):
         remote(
             top.at[pl.ds(0, 1)], top_got.at[d, pl.ds(0, 1)], ts.at[0], tr.at[0], peer
         ).start()
-    halos = halo_copies(0)
-    for copy in halos:
-        copy.start()
     faces(state)
     volume_x(state)
     lax.fori_loop(0, EARLY, functools.partial(early_column, state), 0)

time: 19.1 us -> 18.7 us (0.979)
  Pallas kernels: 18.3 us -> 17.9 us
    pallas_call x1, Pallas kernels: 16.9 us -> 16.6 us  [local(): pl.pallas_call(functools.partial(kernel, ngx, ngy), out_shape=[jax.ShapeD...]
where the time goes in v5:
time: 18.7 us; the launch traced here: 18.6 us
  Pallas kernels  17.9 us (96%)
  between operations  0.64 us (3%)
    pallas_call x1, Pallas kernels, local(): pl.pallas_call(functools.partial(kernel, ngx, ngy), out_shape=[jax.ShapeD...  16.6 us
    pallas_call x1, Pallas kernels, local(): pl.pallas_call(last_kernel, out_shape=(jax.ShapeDtypeStruct(shape, F32),)...  1.3 us

profile of v5, /device:TPU:0, one launch (start us, length us, event | category | flops | bytes accessed | tf_op | source)
XLA Modules:
  0.0 18.6 jit_solution(5144267715669246785)
XLA Ops:
  0.6 16.6 %dg_sections.1 = (f32[4,25,16,128]{3,2,1,0:T(8,128)S(1)}, f32[8,25,16,128]{3,2,1,0:T(8,128)S(1)}, f32[4,25,16,128]{3,2,1,0:T(8,128)S(1)}, f32[4,25,16,128]{3,2,1...) custom-call(f32[4,25,16,128]{3,2,1,0:T(8,128)} %bitcast.1), custom_call_target="tpu_custom_call" | custom-call | tf_op jit(solution)/shard_map/dg_sections/pallas_call | solution.py:513
  17.3 1.3 %dg_last_pass.1 = (f32[4,5,5,16,128]{4,3,2,1,0:T(8,128)}, f32[4,5,5,16,128]{4,3,2,1,0:T(8,128)}) custom-call(f32[4,25,16,128]{3,2,1,0:T(8,128)S(1)} %get-tuple-element.10.state, f32[8,25,16,128]{3,2,1,0:T(8,128)S(1)} %get-tuple-element.11.prim, f32[4,25,16,128]{3,2,1,0:T(8,128)S(1)} %get-tuple-element.12.first, f32[4,25,16,128]{3,2,1,0:T(8,128)S(1)} %get-tuple-element.13.rx, ...), custom_call_target="tpu_custom_call" | custom-call | tf_op jit(solution)/shard_map/dg_last_pass/pallas_call | solution.py:532
